TPU v7x, 32 devices: a whole 2x2x4 slice. The times are simulated.
32 devices in a mesh: grp: 2 (over x), seq: 16 (over z, y, core).
Axes of the slice: x: 2, y: 2, z: 4, core: 2. Of those that a mesh axis runs over, the one named last changes fastest.
Arguments:
- conv_input: bfloat16 [8192, 4352], P(('grp', 'seq')), parts along dimension 0, may hold values from -6 to 6, as said below
- conv_weight: float32 [4, 4352], replicated, may hold values from -3 to 3
- step_logit: float32 [8192, 32], P(('grp', 'seq')), parts along dimension 0, may hold values from -20 to 0, as said below
- decay_log: float32 [32], replicated, may hold values from -0.5 to 0.5
- skip_gain: float32 [32], replicated, may hold values from 0.5 to 2
Outputs:
- mixer_out: bfloat16 [8192, 4096], P(('grp', 'seq')), parts along dimension 0
There are 2 independent parts, one for each index of `grp`. A program takes and returns all parts, laid end to end along the dimension named above; an argument that names none is the same for every part. Nothing has to cross between parts.
Inputs may be any that keep to these rules, and one draw needn't show every extreme that they name: `conv_input`: activations before the convolution. `step_logit`: step sizes before softplus.
All inputs are finite; a program needn't handle non-finite values.
Results may differ from a plain program's by a relative error of at most 0.0047.
Values may be sent and summed in bfloat16 or wider, within the bound.
A program may use at most 128 MiB of HBM per device.

v0:
```python
import jax
import jax.numpy as jnp
from jax import lax
from jax.sharding import PartitionSpec as P

HEADDIM = 128
STATE = 128
GROUP = 256


def as_sent(shard):

    def short(part):
        return part.astype(jnp.bfloat16) if part.dtype == jnp.float32 else part

    return jax.tree.map(short, shard)


def from_behind(value, axis, steps):
    count = lax.axis_size(axis)
    leading, last = (max(0, -steps), min(count, count - steps))
    return lax.ppermute(value, axis, [(source, source + steps) for source in range(leading, last)])


def conv_activate(extended, kernel, row_count):
    running = kernel[0] * extended[0:row_count].astype(jnp.float32)
    for tap_index in range(1, kernel.shape[0]):
        running = running + kernel[tap_index] * extended[tap_index : tap_index + row_count].astype(
            jnp.float32
        )
    return jax.nn.silu(running).astype(jnp.bfloat16)


def group_terms(activated, logits, decay_rate, skip_gain):
    head_count = decay_rate.shape[0]
    inner_width = head_count * HEADDIM
    block_count = activated.shape[0]
    span_rows = activated.shape[1]
    values = activated[:, :, :inner_width].reshape(block_count, span_rows, head_count, HEADDIM)
    b_rows = activated[:, :, inner_width : inner_width + STATE]
    c_rows = activated[:, :, inner_width + STATE :]
    time_step_size = jax.nn.softplus(logits)
    cum_decay = jnp.cumsum(time_step_size * decay_rate, axis=1)
    decay_t = jnp.transpose(cum_decay, (0, 2, 1))
    step_t = jnp.transpose(time_step_size, (0, 2, 1))
    scores = jnp.einsum("cqn,csn->cqs", c_rows, b_rows, preferred_element_type=jnp.float32)
    token_position = jnp.arange(span_rows)
    causal = token_position[:, None] >= token_position[None, :]
    decay_gap = jnp.where(causal, decay_t[:, :, :, None] - decay_t[:, :, None, :], -jnp.inf)
    weights = (scores[:, None] * jnp.exp(decay_gap) * step_t[:, :, None, :]).astype(jnp.bfloat16)
    intra_out = jnp.einsum("chqs,cshp->cqhp", weights, values, preferred_element_type=jnp.float32)
    local_out = intra_out + skip_gain[:, None] * values.astype(jnp.float32)
    tail_weight = jnp.transpose(jnp.exp(decay_t[:, :, -1:] - decay_t) * step_t, (0, 2, 1))
    weighted = (values * tail_weight[..., None]).astype(jnp.bfloat16)
    states = jnp.einsum("cshp,csn->chpn", weighted, b_rows, preferred_element_type=jnp.float32)
    return (local_out, states, cum_decay, c_rows)


def split_parts(state_field):
    upper_part = lax.optimization_barrier(state_field.astype(jnp.bfloat16))
    lower_part = (state_field - upper_part.astype(jnp.float32)).astype(jnp.bfloat16)
    return (upper_part, lower_part)


def state_readout(form, c_rows, state_field):
    upper_part, lower_part = split_parts(state_field)
    upper_term = jnp.einsum(form, c_rows, upper_part, preferred_element_type=jnp.float32)
    lower_term = jnp.einsum(form, c_rows, lower_part, preferred_element_type=jnp.float32)
    return upper_term + lower_term


def chain_states(initial, group_ends, states):

    def advance(current, pieces):
        end_log, piece = pieces
        return (jnp.exp(end_log)[:, None, None] * current + piece, current)

    final_state, entering = lax.scan(advance, initial, (group_ends, states))
    return (entering, final_state)


def carry_state(device_log, final_state):
    head_count = device_log.shape[0]
    all_logs = lax.all_gather(device_log[None, :], "seq", axis=0, tiled=True)
    flat_state = final_state.reshape(1, head_count * HEADDIM, STATE)
    received = lax.all_to_all(
        flat_state.astype(jnp.bfloat16), "seq", split_axis=1, concat_axis=0, tiled=True
    ).astype(flat_state.dtype)
    source_count = received.shape[0]
    row_count = received.shape[1]
    first_row = lax.axis_index("seq") * row_count
    head_of = (first_row + jnp.arange(row_count, dtype=jnp.int32)) // HEADDIM
    head_pick = (head_of[:, None] == jnp.arange(head_count, dtype=jnp.int32)[None, :]).astype(
        jnp.float32
    )
    row_logs = jnp.dot(all_logs, head_pick.T, precision=lax.Precision.HIGHEST)
    total_log = jnp.cumsum(row_logs, axis=0)
    before_log = total_log - row_logs
    source_order = jnp.arange(source_count)
    earlier_mask = source_order[None, :] < source_order[:, None]
    exponent = jnp.where(
        earlier_mask[:, :, None], before_log[:, None, :] - total_log[None, :, :], -jnp.inf
    )
    mixed = jnp.einsum("sjr,jrn->srn", jnp.exp(exponent), received, precision=lax.Precision.HIGHEST)
    returned = lax.all_to_all(
        as_sent(mixed), "seq", split_axis=0, concat_axis=1, tiled=True
    ).astype(mixed.dtype)
    return returned.reshape(head_count, HEADDIM, STATE)


def on_device(conv_input, conv_weight, step_logit, decay_log, skip_gain):
    tap_count = conv_weight.shape[0]
    row_count = conv_input.shape[0]
    edge_rows = conv_input[row_count - (tap_count - 1) :]
    previous = from_behind(edge_rows, "seq", 1)
    extended = jnp.concatenate([previous, conv_input], 0)
    block_count = row_count // GROUP
    activated = conv_activate(extended, conv_weight, row_count).reshape(block_count, GROUP, -1)
    logits = step_logit.reshape(block_count, GROUP, -1)
    decay_rate = -jnp.exp(decay_log)
    local_out, states, cum_decay, c_rows = group_terms(activated, logits, decay_rate, skip_gain)
    group_ends = cum_decay[:, -1, :]
    device_log = jnp.sum(group_ends, axis=0)
    empty_state = jnp.zeros_like(states[0])
    _, final_state = chain_states(empty_state, group_ends, states)
    incoming = carry_state(device_log, final_state)
    entering, _ = chain_states(incoming, group_ends, states)
    inter_out = jnp.exp(cum_decay)[..., None] * state_readout("cqn,chpn->cqhp", c_rows, entering)
    result = local_out + inter_out
    return result.reshape(row_count, -1).astype(jnp.bfloat16)


def solution(mesh):
    return jax.shard_map(
        on_device,
        mesh=mesh,
        in_specs=(P(("grp", "seq"), None), P(), P(("grp", "seq"), None), P(), P()),
        out_specs=P(("grp", "seq"), None),
        check_vma=False,
    )
```

profile of v0, /device:TPU:25, one launch (start us, length us, event | category | flops | bytes accessed | tf_op | source)
XLA Modules:
  0.0 159.0 jit_solution(3897748167165078665)
XLA Ops:
  0.0 0.9 slice.46
  0.9 3.7 %collective-permute-start = (bf16[3,4352]{1,0:T(4,128)(2,1)S(1)}, bf16[3,4352]{1,0:T(4,128)(2,1)S(1)}, u32[]{:S(2)}, u32[]{:S(2)}) collective-permute-start(bf16[3,4352]{1,0:T(4,128)(2,1)S(1)} %slice.46), channel_id=1, source_target_pairs={{0,1},{1,2},{2,3},{3,4},{4,5},{5,6},{6,7},{7,8},{8,9},{9,10},{10,1... | collective-permute-start | bytes 78344 | tf_op jit(solution)/shard_map/ppermute | solution.py:22
  8.4 1.2 slice_reduce_fusion.4
  9.7 2.5 %mul.190 = f32[256,32,128]{2,1,0:T(8,128)} broadcast(f32[256,32]{1,0:T(8,128)S(1)} %bitcast.104), dimensions={0,1} | broadcast | bytes 4227072 | tf_op jit(solution)/shard_map/mul | solution.py:54
  12.3 5.0 %mul.191 = f32[1,256,4096]{2,1,0:T(8,128)} reshape(f32[256,32,128]{2,1,0:T(8,128)} %mul.190) | data formatting | bytes 8388608 | tf_op jit(solution)/shard_map/mul | solution.py:54
  17.3 6.1 %fusion.13 = bf16[1,256,4352]{2,1,0:T(8,128)(2,1)S(1)} fusion(bf16[256,4352]{1,0:T(8,128)(2,1)} %param.5, f32[4352]{0:T(1024)S(1)} %get-tuple-element.27, bf16[3,4352]{1,0:T(4,128)(2,1)S(1)} %collective-permute-done, f32[4352]{0:T(1024)S(1)} %get-tuple-element.28, f32[4352]{0:T(1024)S(1)} %get-tuple-element.26, f32[4352]{0:T(1024)S(1)} %get-tuple-element.20), kind=kLoop, calls=%fused_computation.21 | loop fusion | flops 27852800 | bytes 4552192 | tf_op jit(solution)/shard_map/reshape | solution.py:118
  24.5 3.0 %fusion.1 = bf16[1,4096,128]{2,1,0:T(8,128)(2,1)S(1)} fusion(bf16[32,8,32,128]{3,2,1,0:T(8,128)(2,1)S(1)} %copy.62, f32[4096]{0:T(1024)S(1)} %broadcast_bitcast_fusion, bf16[1,256,4352]{2,1,0:T(8,128)(2,1)S(1)} %fusion.13), kind=kOutput, calls=%fused_computation.3 | convolution fusion | flops 269484032 | bytes 3227648 | tf_op jit(solution)/shard_map/cshp,csn->chpn/dot_general | solution.py:55
  27.5 17.0 %copy.79 = bf16[1,4096,128]{2,0,1:T(2,128)(2,1)} copy(bf16[1,4096,128]{2,1,0:T(8,128)(2,1)S(1)} %fusion.1) | data formatting | bytes 2097152 | tf_op jit(solution)/shard_map/convert_element_type | solution.py:87
  45.1 23.7 %reduce.14 = bf16[4096,128]{1,0:T(8,128)(2,1)S(1)} reduce(bf16[4096,1,128]{2,1,0:T(2,128)(2,1)} %bitcast.99, bf16[]{:T(256)} %broadcast.138), dimensions={1}, to_apply=%bitcast.95.reduce_sub_computation | reduce | bytes 2097154
  68.8 1.1 reshape.321
  69.9 4.9 %all-to-all-start = ((bf16[16,2,16384]{2,1,0:T(2,128)(2,1)}), bf16[16,2,16384]{2,1,0:T(2,128)(2,1)S(1)}, u32[]{:S(2)}, u32[]{:S(2)}) async-start(bf16[16,2,16384]{2,1,0:T(2,128)(2,1)} %reshape.321), calls=%async_computation | async-start | bytes 2097152 | tf_op jit(solution)/shard_map/all_to_all | solution.py:86
  74.8 34.1 %all-gather = f32[16,1,32]{2,1,0:T(1,128)S(1)} all-gather(f32[1,1,32]{2,1,0:T(1,128)S(1)} %copy.49), channel_id=2, replica_groups=mesh['grp'=2,'seq'=16] {'seq'}, dimensions={0}, use_global_device_ids=true | all-gather | bytes 2176 | tf_op jit(solution)/shard_map/all_gather | solution.py:84
  110.0 1.5 copy.50
  111.4 3.4 %reshape.322 = bf16[4096,1,128]{2,1,0:T(2,128)(2,1)} reshape(bf16[16,2,16384]{2,1,0:T(2,128)(2,1)S(1)} %all-to-all-done) | data formatting | bytes 2097152
  114.9 1.7 %copy.58 = bf16[1,4096,128]{2,1,0:T(8,128)(2,1)S(1)} copy(bf16[1,4096,128]{2,0,1:T(2,128)(2,1)} %bitcast.98) | data formatting | bytes 2097152
  116.6 3.9 %fusion.24 = bf16[16,256,128]{2,0,1:T(8,128)(2,1)S(1)} fusion(bf16[16,256,128]{2,1,0:T(8,128)(2,1)S(1)} %bitcast.103, f32[16,256]{0,1:T(8,128)S(1)} %copy.51, f32[16,256]{0,1:T(8,128)} %copy.50, pred[16,16]{1,0:T(8,128)(4,1)S(1)} %iota_compare_fusion.3), kind=kOutput, calls=%fused_computation.31 | convolution fusion | flops 101318656 | bytes 2130176 | tf_op jit(solution)/shard_map/sjr,jrn->srn/dot_general | solution.py:104
  120.5 1.2 copy.53
  121.8 5.0 %all-to-all-start.1 = ((bf16[16,256,128]{2,1,0:T(8,128)(2,1)}), bf16[16,256,128]{2,1,0:T(8,128)(2,1)S(1)}, u32[]{:S(2)}, u32[]{:S(2)}) async-start(bf16[16,256,128]{2,1,0:T(8,128)(2,1)} %copy.53), calls=%async_computation.1 | async-start | bytes 2097152 | tf_op jit(solution)/shard_map/all_to_all | solution.py:105
  129.4 3.2 %fusion.48 = (bf16[1,256,4096]{2,1,0:T(8,128)(2,1)}, f32[1,256,4096]{2,1,0:T(8,128)}) fusion(bf16[1,256,4352]{2,1,0:T(8,128)(2,1)S(1)} %fusion.13), kind=kLoop, calls=%fused_computation.80 | loop fusion | flops 1048576 | bytes 8388608 | tf_op jit(solution)/shard_map/slice | solution.py:39
  132.6 4.1 %copy.41 = bf16[1,256,4096]{1,2,0:T(8,128)(2,1)} copy(bf16[1,256,4096]{2,1,0:T(8,128)(2,1)} %get-tuple-element.36) | data formatting | bytes 4194304 | tf_op jit(solution)/shard_map/slice | solution.py:39
  136.6 5.6 %copy.45 = f32[1,256,4096]{1,2,0:T(8,128)} copy(f32[1,256,4096]{2,1,0:T(8,128)} %get-tuple-element.38) | data formatting | bytes 8388608 | tf_op jit(solution)/shard_map/convert_element_type | solution.py:52
  142.4 7.4 %all-to-all-done.1 = bf16[16,256,128]{2,1,0:T(8,128)(2,1)S(1)} async-done(((bf16[16,256,128]{2,1,0:T(8,128)(2,1)}), bf16[16,256,128]{2,1,0:T(8,128)(2,1)S(1)}, u32[]{:S(2)}, u32[]{:S(2)}) %all-to-all-start.1) | async-done | bytes 1048608 | tf_op jit(solution)/shard_map/all_to_all | solution.py:105
  152.8 3.4 %fusion.4 = bf16[1,256,32,128]{1,3,2,0:T(8,128)(2,1)S(1)} fusion(f32[256,32,128]{0,2,1:T(8,128)S(1)} %fusion.30, f32[256,32,128]{0,2,1:T(8,128)S(1)} %fusion.28, f32[1,256,32,128]{1,3,2,0:T(8,128)S(1)} %bitcast.100, f32[256,32]{0,1:T(8,128)S(1)} %bitcast.111, f32[32]{0:T(128)S(1)} %copy-done.7, bf16[256,32,128]{0,2,1:T(8,128)(2,1)S(1)} %bitcast.101, ...), kind=kOutput, calls=%fused_computation.8 | convolution fusion | flops 553648128 | bytes 17203328 | tf_op jit(solution)/shard_map/chqs,cshp->cqhp/dot_general | solution.py:51
  156.2 2.9 %copy.54 = bf16[256,4096]{1,0:T(8,128)(2,1)} copy(bf16[256,4096]{0,1:T(8,128)(2,1)S(1)} %bitcast.102) | data formatting | bytes 4194304 | tf_op jit(solution)/shard_map/convert_element_type | solution.py:130
  (53 shorter events, 12.1 us)
Async XLA Ops:
  0.9 16.4 %collective-permute-start = (bf16[3,4352]{1,0:T(4,128)(2,1)S(1)}, bf16[3,4352]{1,0:T(4,128)(2,1)S(1)}, u32[]{:S(2)}, u32[]{:S(2)}) collective-permute-start(bf16[3,4352]{1,0:T(4,128)(2,1)S(1)} %slice.46), channel_id=1, source_target_pairs={{0,1},{1,2},{2,3},{3,4},{4,5},{5,6},{6,7},{7,8},{8,9},{9,10},{10,1... | collective-permute-start | bytes 78344 | tf_op jit(solution)/shard_map/ppermute | solution.py:22
  17.3 6.1 %copy-start = (f32[1,256,4096]{2,1,0:T(8,128)S(1)}, f32[1,256,4096]{2,1,0:T(8,128)}, u32[]{:S(2)}) copy-start(f32[1,256,4096]{2,1,0:T(8,128)} %mul.191) | copy-start | bytes 12582916
  69.9 41.5 %all-to-all-start = ((bf16[16,2,16384]{2,1,0:T(2,128)(2,1)}), bf16[16,2,16384]{2,1,0:T(2,128)(2,1)S(1)}, u32[]{:S(2)}, u32[]{:S(2)}) async-start(bf16[16,2,16384]{2,1,0:T(2,128)(2,1)} %reshape.321), calls=%async_computation | async-start | bytes 2097152 | tf_op jit(solution)/shard_map/all_to_all | solution.py:86
  121.8 28.1 %all-to-all-start.1 = ((bf16[16,256,128]{2,1,0:T(8,128)(2,1)}), bf16[16,256,128]{2,1,0:T(8,128)(2,1)S(1)}, u32[]{:S(2)}, u32[]{:S(2)}) async-start(bf16[16,256,128]{2,1,0:T(8,128)(2,1)} %copy.53), calls=%async_computation.1 | async-start | bytes 2097152 | tf_op jit(solution)/shard_map/all_to_all | solution.py:105
  149.9 2.2 %copy-start.1 = (f32[1,256,4096]{1,2,0:T(8,128)S(1)}, f32[1,256,4096]{1,2,0:T(8,128)}, u32[]{:S(2)}) copy-start(f32[1,256,4096]{1,2,0:T(8,128)} %copy.45) | copy-start | bytes 12582916
  149.9 2.9 %copy-start.2 = (bf16[1,256,4096]{1,2,0:T(8,128)(2,1)S(1)}, bf16[1,256,4096]{1,2,0:T(8,128)(2,1)}, u32[]{:S(2)}) copy-start(bf16[1,256,4096]{1,2,0:T(8,128)(2,1)} %copy.41) | copy-start | bytes 6291460
  149.9 2.9 %copy-start.3 = (pred[256,256]{1,0:T(8,128)(4,1)S(1)}, pred[256,256]{1,0:T(8,128)(4,1)}, u32[]{:S(2)}) copy-start(pred[256,256]{1,0:T(8,128)(4,1)} %iota_compare_fusion) | copy-start | bytes 196612
  149.9 2.9 %copy-start.4 = (f32[32,256]{1,0:T(8,128)S(1)}, f32[32,256]{1,0:T(8,128)}, u32[]{:S(2)}) copy-start(f32[32,256]{1,0:T(8,128)} %bitcast_add_fusion.1) | copy-start | bytes 98308
  149.9 2.9 %copy-start.5 = (f32[1,256,32]{1,2,0:T(8,128)S(1)}, f32[1,256,32]{1,2,0:T(8,128)}, u32[]{:S(2)}) copy-start(f32[1,256,32]{1,2,0:T(8,128)} %copy.77) | copy-start | bytes 98308
  149.9 2.9 %copy-start.6 = (f32[1,32,256]{2,1,0:T(8,128)S(1)}, f32[1,32,256]{2,1,0:T(8,128)}, u32[]{:S(2)}) copy-start(f32[1,32,256]{2,1,0:T(8,128)} %copy.78) | copy-start | bytes 98308
  149.9 2.9 %copy-start.7 = (f32[32]{0:T(128)S(1)}, f32[32]{0:T(128)}, u32[]{:S(2)}) copy-start(f32[32]{0:T(128)} %param.9) | copy-start | bytes 388
where the time goes:
time: 162 us; the launch traced here: 159 us
  local copies, waits for them, and re-layouts  53.2 us (33%)
  other arithmetic  38.3 us (24%)
  blocking collectives  34.1 us (21%)
  starting transfers between devices  13.6 us (8%)
  matrix products  12.2 us (8%)
  waiting for transfers between devices  7.45 us (5%)
    all_gather x1, blocking collectives, carry_state(): all_logs = lax.all_gather(device_log[None, :], 'seq', axis=0, tiled=True)  34.1 us
    unnamed x2, other arithmetic  24.2 us
    convert_element_type x1, local copies, waits for them, and re-layouts, carry_state(): flat_state.astype(jnp.bfloat16)  17 us
    unnamed x23, local copies, waits for them, and re-layouts  9.99 us
    mul x3, local copies, waits for them, and re-layouts, group_terms(): weighted = (values * tail_weight[..., None]).astype(jnp.bfloat16)  7.62 us
    all_to_all x1, waiting for transfers between devices, carry_state(): lax.all_to_all(as_sent(mixed), 'seq', split_axis=0, concat_axis=1, tiled=...  7.44 us
    reshape x1, other arithmetic, on_device(): conv_activate(extended, conv_weight, row_count)  6.12 us
    convert_element_type x1, local copies, waits for them, and re-layouts, group_terms(): local_out = intra_out + skip_gain[:, None] * values.astype(jnp.float32)  5.6 us
  transfers between devices with their start and end apart: 3, of which 1 were waited for; matrix products, arithmetic and copies ran while one was open for 19% of the time, Pallas kernels for 0%

commit v1 on v0

v1 whole, which is shorter than its diff:
```python
import functools

import jax
import jax.numpy as jnp
from jax import lax
from jax.experimental import pallas as pl
from jax.experimental.pallas import tpu as pltpu
from jax.sharding import PartitionSpec as P

HEADDIM = 128
STATE = 128
PAIR = 2 * HEADDIM
MESH = pl.DeviceIdType.MESH
F32 = jnp.float32
BF16 = jnp.bfloat16


def softplus(x):
    e = jnp.exp(-jnp.abs(x))
    series = e * (1.0 - e * (1 / 2 - e * (1 / 3 - e * (1 / 4 - e * (1 / 5 - e * (1 / 6))))))
    return jnp.maximum(x, 0.0) + jnp.where(e < 0.03, series, jnp.log(1.0 + e))


def kernel(
    n_seq, heads, rows, taps,
    x_ref, w_ref, sl_ref, dl_ref, skip_ref, out_ref,
    halo, ext, act, b_t, c_act, scores, tail_tab, cum_tab, rowg, tot,
    s_send, s_own, s_recv, t_own, t_send, t_recv, p_send, p_recv, e_send, e_recv, ent, local,
    halo_sems, tot_sems, s_sems, t_sems, p_sems, e_sems,
):
    me = lax.axis_index("seq")
    grp = lax.axis_index("grp")
    core = me % 2
    side = (me // 2) % 2
    quad = me // 4
    quads = n_seq // 4
    place = me % 4
    half = heads // 4
    inner = heads * HEADDIM
    has_next = quad < quads - 1
    has_prev = quad > 0

    def xor_peer(r):
        flip_core = (1 - 2 * core) * (r % 2)
        flip_side = (1 - 2 * side) * (r // 2) * 2
        return me + flip_core + flip_side

    def dev(seq_index):
        return (grp, seq_index)

    barrier = pltpu.get_barrier_semaphore()
    for r in (1, 2, 3):
        pl.semaphore_signal(barrier, inc=1, device_id=dev(xor_peer(r)), device_id_type=MESH)

    @pl.when(has_next)
    def _():
        pl.semaphore_signal(barrier, inc=1, device_id=dev(me + 4), device_id_type=MESH)

        @pl.when(place == 3)
        def _():
            pl.semaphore_signal(barrier, inc=1, device_id=dev(me + 1), device_id_type=MESH)

    @pl.when(has_prev)
    def _():
        pl.semaphore_signal(barrier, inc=1, device_id=dev(me - 4), device_id_type=MESH)

        @pl.when(place == 0)
        def _():
            pl.semaphore_signal(barrier, inc=1, device_id=dev(me - 1), device_id_type=MESH)

    next_count = 1 - (quad + 1) // quads
    prev_count = (quad + quads - 1) // quads
    pl.semaphore_wait(
        barrier,
        3 + next_count * (1 + place // 3) + prev_count * (2 - (place + 3) // 4),
    )

    def remote(src, dst, sems, j, target):
        return pltpu.make_async_remote_copy(
            src_ref=src, dst_ref=dst, send_sem=sems.at[0, j], recv_sem=sems.at[1, j],
            device_id=dev(target), device_id_type=MESH,
        )

    def halo_copy():
        return remote(x_ref.at[pl.ds(rows - 16, 16)], halo, halo_sems, 0, me + 1)

    @pl.when(me < n_seq - 1)
    def _():
        halo_copy().start()

    step = softplus(sl_ref[...])
    eye = lax.broadcasted_iota(jnp.int32, (heads, heads), 0) == lax.broadcasted_iota(
        jnp.int32, (heads, heads), 1
    )
    rate = jnp.sum(jnp.where(eye, -jnp.exp(dl_ref[...]), 0.0), axis=1, keepdims=True)
    row_id = lax.broadcasted_iota(jnp.int32, (rows, rows), 0)
    col_id = lax.broadcasted_iota(jnp.int32, (rows, rows), 1)
    upto = (row_id <= col_id).astype(F32)
    cum_t = jnp.dot(
        step * rate, upto, preferred_element_type=F32, precision=lax.Precision.HIGHEST
    )
    cum_end = cum_t[:, rows - 1 : rows]
    for h in range(heads):
        tot[0, h // 2 : h // 2 + 1, pl.ds((h % 2) * HEADDIM, HEADDIM)] = jnp.broadcast_to(
            cum_end[h : h + 1, :], (1, HEADDIM)
        )
    for r in (1, 2, 3):
        remote(tot.at[0], tot.at[r], tot_sems, r, xor_peer(r)).start()
    rowg[...] = cum_t - jnp.log(step)
    cum = jnp.transpose(cum_t)
    tail = jnp.transpose(jnp.exp(cum_end - cum_t) * step)
    for h in range(heads):
        tail_tab[h] = jnp.broadcast_to(tail[:, h : h + 1], (rows, HEADDIM))
        cum_tab[h] = jnp.broadcast_to(cum[:, h : h + 1], (rows, HEADDIM))

    @pl.when(me == 0)
    def _():
        halo[...] = jnp.zeros_like(halo)

    @pl.when(me > 0)
    def _():
        halo_copy().wait_recv()

    def conv(start, slot):
        cols = pl.ds(start, PAIR)
        ext[slot, 0:8, :] = halo[:, cols].astype(F32)[8:16]
        ext[slot, 8 : 8 + rows, :] = x_ref[:, cols].astype(F32)
        total = w_ref[0:1, cols] * ext[slot, pl.ds(9 - taps, rows), :]
        for k in range(1, taps):
            total = total + w_ref[k : k + 1, cols] * ext[slot, pl.ds(9 - taps + k, rows), :]
        half_v = 0.5 * total
        return (half_v + half_v * jnp.tanh(half_v)).astype(BF16)

    maps = conv(inner, 0)
    b_rows = maps[:, :STATE]
    c_rows = maps[:, STATE:]
    b_trans = jnp.transpose(b_rows.astype(F32)).astype(BF16)
    b_t[...] = b_trans
    c_act[...] = c_rows
    raw = jnp.dot(c_rows, b_trans, preferred_element_type=F32)
    scores[...] = jnp.where(row_id >= col_id, raw, 0.0)

    own_first = half * core
    other_first = half * (1 - core)

    def pair_state(i, slot):
        a = conv(pl.multiple_of(i * PAIR, PAIR), slot)
        act[i] = a
        left = a[:, :HEADDIM].astype(F32) * tail_tab[2 * i]
        right = a[:, HEADDIM:].astype(F32) * tail_tab[2 * i + 1]
        weighted = jnp.concatenate([left.astype(BF16), right.astype(BF16)], axis=1)
        return jnp.dot(b_t[...], weighted, preferred_element_type=F32)

    def s_copy(j):
        return remote(s_send.at[j], s_recv.at[j], s_sems, j, xor_peer(1))

    def t_copy(j):
        return remote(t_send.at[j], t_recv.at[j], t_sems, j, xor_peer(2))

    def p_copy(j):
        return remote(p_send.at[j], p_recv.at[j], p_sems, j, me + 4)

    def e_copy(j):
        return remote(e_send.at[j], e_recv.at[j], e_sems, j, xor_peer(1))

    def logs(r, j):
        return tot[r, pl.ds(own_first + j, 1), :]

    def first_state(j):
        return jnp.where(core == 0, s_own[j], s_recv[j].astype(F32))

    def chip_step(j):
        s_copy(j).wait_recv()
        mine, got = s_own[j], s_recv[j].astype(F32)
        decay_last = jnp.exp(jnp.where(core == 0, logs(1, j), logs(0, j)))
        total = decay_last * jnp.where(core == 0, mine, got) + jnp.where(core == 0, got, mine)
        t_own[j] = total
        t_send[j] = total.astype(BF16)
        t_copy(j).start()

    for r in (1, 2, 3):
        remote(tot.at[0], tot.at[r], tot_sems, r, xor_peer(r)).wait_recv()

    @pl.loop(0, half)
    def _(j):
        s_send[j] = pair_state(other_first + j, 0).astype(BF16)
        s_copy(j).start()
        s_own[j] = pair_state(own_first + j, 1)

        @pl.when(j >= 1)
        def _():
            chip_step(j - 1)

    chip_step(half - 1)

    def quad_step(j):
        t_copy(j).wait_recv()
        mine, got = t_own[j], t_recv[j].astype(F32)
        log_mine = logs(0, j) + logs(1, j)
        log_got = logs(2, j) + logs(3, j)
        log_0 = jnp.where(side == 0, log_mine, log_got)
        log_1 = jnp.where(side == 0, log_got, log_mine)
        t_0 = jnp.where(side == 0, mine, got)
        t_1 = jnp.where(side == 0, got, mine)
        plane = jnp.exp(log_1) * t_0 + t_1

        @pl.when(has_prev)
        def _():
            p_copy(j).wait_recv()

        @pl.when(quad == 0)
        def _():
            p_recv[j] = jnp.zeros((STATE, PAIR), BF16)

        before = p_recv[j].astype(F32)

        @pl.when(has_next)
        def _():
            p_send[j] = (jnp.exp(log_0 + log_1) * before + plane).astype(BF16)
            p_copy(j).start()

        e_chip = jnp.where(side == 0, before, jnp.exp(log_0) * before + t_0)
        decay_first = jnp.exp(jnp.where(core == 0, logs(0, j), logs(1, j)))
        e_second = decay_first * e_chip + first_state(j)
        e_send[j] = jnp.where(core == 0, e_second, e_chip).astype(BF16)
        e_copy(j).start()
        ent[j] = jnp.where(core == 0, e_chip, e_second).astype(BF16)

    mid = rows // 2

    def intra(i):
        for u in range(2):
            h = 2 * i + u
            lanes = pl.ds(u * HEADDIM, HEADDIM)
            g = rowg[pl.ds(h, 1), :]
            col = cum_tab[h]
            v = act[i, :, lanes]
            gain = skip_ref[h]
            top = scores[0:mid, 0:mid] * jnp.exp(jnp.minimum(col[:mid] - g[:, :mid], 0.0))
            low_a = scores[mid:, 0:mid] * jnp.exp(jnp.minimum(col[mid:] - g[:, :mid], 0.0))
            low_b = scores[mid:, mid:] * jnp.exp(jnp.minimum(col[mid:] - g[:, mid:], 0.0))
            low = jnp.concatenate([low_a.astype(BF16), low_b.astype(BF16)], axis=1)
            y_top = jnp.dot(top.astype(BF16), v[:mid], preferred_element_type=F32)
            y_low = jnp.dot(low, v, preferred_element_type=F32)
            local[i, 0:mid, lanes] = y_top + gain * v[:mid].astype(F32)
            local[i, mid:, lanes] = y_low + gain * v[mid:].astype(F32)

    def finish(i, state):
        inter = jnp.dot(c_act[...], state, preferred_element_type=F32)
        grow = jnp.concatenate([jnp.exp(cum_tab[2 * i]), jnp.exp(cum_tab[2 * i + 1])], axis=1)
        out_ref[:, pl.ds(pl.multiple_of(i * PAIR, PAIR), PAIR)] = (
            local[i] + grow * inter
        ).astype(out_ref.dtype)

    def finish_step(j):
        finish(own_first + j, ent[j])
        e_copy(j).wait_recv()
        finish(other_first + j, e_recv[j])

    @pl.loop(0, half)
    def _(j):
        quad_step(j)
        intra(own_first + j)
        intra(other_first + j)

        @pl.when(j >= 1)
        def _():
            finish_step(j - 1)

    finish_step(half - 1)

    @pl.when(me < n_seq - 1)
    def _():
        halo_copy().wait_send()

    for r in (1, 2, 3):
        remote(tot.at[0], tot.at[r], tot_sems, r, xor_peer(r)).wait_send()

    @pl.loop(0, half)
    def _(j):
        s_copy(j).wait_send()
        t_copy(j).wait_send()
        e_copy(j).wait_send()

        @pl.when(has_next)
        def _():
            p_copy(j).wait_send()


def on_device(n_seq, conv_input, conv_weight, step_logit, decay_log, skip_gain):
    taps, channels = conv_weight.shape
    rows = conv_input.shape[0]
    heads = decay_log.shape[0]
    half = heads // 4
    vmem = pl.BlockSpec(memory_space=pltpu.VMEM)
    chunk = (half, STATE, PAIR)

    def pair_sems(count):
        return pltpu.SemaphoreType.DMA((2, count))

    return pl.pallas_call(
        functools.partial(kernel, n_seq, heads, rows, taps),
        out_shape=jax.ShapeDtypeStruct((rows, heads * HEADDIM), BF16),
        in_specs=[vmem, vmem, vmem, vmem, pl.BlockSpec(memory_space=pltpu.SMEM)],
        out_specs=vmem,
        scratch_shapes=[
            pltpu.VMEM((16, channels), BF16),
            pltpu.VMEM((2, rows + 8, PAIR), F32),
            pltpu.VMEM((heads // 2, rows, PAIR), BF16),
            pltpu.VMEM((STATE, rows), BF16),
            pltpu.VMEM((rows, STATE), BF16),
            pltpu.VMEM((rows, rows), F32),
            pltpu.VMEM((heads, rows, HEADDIM), F32),
            pltpu.VMEM((heads, rows, HEADDIM), F32),
            pltpu.VMEM((heads, rows), F32),
            pltpu.VMEM((4, heads // 2, PAIR), F32),
            pltpu.VMEM(chunk, BF16),
            pltpu.VMEM(chunk, F32),
            pltpu.VMEM(chunk, BF16),
            pltpu.VMEM(chunk, F32),
            pltpu.VMEM(chunk, BF16),
            pltpu.VMEM(chunk, BF16),
            pltpu.VMEM(chunk, BF16),
            pltpu.VMEM(chunk, BF16),
            pltpu.VMEM(chunk, BF16),
            pltpu.VMEM(chunk, BF16),
            pltpu.VMEM(chunk, BF16),
            pltpu.VMEM((heads // 2, rows, PAIR), F32),
            pair_sems(1),
            pair_sems(4),
            pair_sems(half),
            pair_sems(half),
            pair_sems(half),
            pair_sems(half),
        ],
        compiler_params=pltpu.CompilerParams(
            collective_id=0, has_side_effects=True, vmem_limit_bytes=48 * 1024 * 1024
        ),
    )(conv_input, conv_weight, step_logit.T, decay_log.reshape(1, heads), skip_gain)


def solution(mesh):
    return jax.shard_map(
        functools.partial(on_device, mesh.shape["seq"]),
        mesh=mesh,
        in_specs=(P(("grp", "seq"), None), P(), P(("grp", "seq"), None), P(), P()),
        out_specs=P(("grp", "seq"), None),
        check_vma=False,
    )
```

time: 162 us -> 41.2 us (0.25); the launches traced: 159 us -> 41 us
  local copies, waits for them, and re-layouts: 53.2 us -> 5.9 us
  other arithmetic: 38.3 us -> 0 us
  Pallas kernels: 0 us -> 35.1 us
  blocking collectives: 34.1 us -> 0 us
  starting transfers between devices: 13.6 us -> 0 us
  matrix products: 12.2 us -> 0 us
  waiting for transfers between devices: 7.45 us -> 0 us
    pallas_call x0 -> x1, Pallas kernels: none -> 35.1 us  [on_device(): pl.pallas_call(functools.partial(kernel, n_seq, heads, rows, taps), out_s...]
    all_gather x1 -> x0, blocking collectives: 34.1 us -> none  [carry_state(): all_logs = lax.all_gather(device_log[None, :], 'seq', axis=0, tiled=True)]
    convert_element_type x4 -> x0, local copies, waits for them, and re-layouts: 26.7 us -> none  [the longest x1 17 us: carry_state(): flat_state.astype(jnp.bfloat16)]
    unnamed x2 -> x0, other arithmetic: 24.2 us -> none
    dot_general x7 -> x0, matrix products: 12.2 us -> none  [the longest x1 3.94 us: carry_state(): jnp.einsum('sjr,jrn->srn', jnp.exp(exponent), received, precision=lax.Pre...]
    all_to_all x2 -> x0, starting transfers between devices: 9.92 us -> none  [the longest x1 5.04 us: carry_state(): lax.all_to_all(as_sent(mixed), 'seq', split_axis=0, concat_axis=1, tiled=...]
    mul x4 -> x0, local copies, waits for them, and re-layouts: 7.69 us -> none  [the longest x3 7.62 us: group_terms(): weighted = (values * tail_weight[..., None]).astype(jnp.bfloat16)]
    all_to_all x2 -> x0, waiting for transfers between devices: 7.44 us -> none  [the longest x1 7.44 us: carry_state(): lax.all_to_all(as_sent(mixed), 'seq', split_axis=0, concat_axis=1, tiled=...]
  transfers between devices with their start and end apart: 3 -> 0, of which waited for: 1 -> 0; matrix products, arithmetic and copies ran while one was open for 19% -> 0% of each run, Pallas kernels for 0% -> 0%
where the time goes in v1:
time: 41.2 us; the launch traced here: 41 us
  Pallas kernels  35.1 us (85%)
  local copies, waits for them, and re-layouts  5.9 us (14%)
    pallas_call x1, Pallas kernels, on_device(): pl.pallas_call(functools.partial(kernel, n_seq, heads, rows, taps), out_s...  35.1 us
    unnamed x11, local copies, waits for them, and re-layouts  5.9 us

profile of v1, /device:TPU:25, one launch (start us, length us, event | category | flops | bytes accessed | tf_op | source)
XLA Modules:
  0.0 41.0 jit_solution(8048188351651452960)
XLA Ops:
  0.0 0.0 copy-start
  0.0 1.6 %copy-done = bf16[256,4352]{1,0:T(8,128)(2,1)S(1)} copy-done((bf16[256,4352]{1,0:T(8,128)(2,1)S(1)}, bf16[256,4352]{1,0:T(8,128)(2,1)}, u32[]{:S(2)}) %copy-start) | copy-done | bytes 2228248
  1.6 0.0 copy-start.1
  1.6 0.9 %copy-done.1 = f32[4,4352]{1,0:T(4,128)S(1)} copy-done((f32[4,4352]{1,0:T(4,128)S(1)}, f32[4,4352]{1,0:T(4,128)}, u32[]{:S(2)}) %copy-start.1) | copy-done | bytes 69656
  2.5 0.0 copy-start.2
  2.5 0.8 %copy-done.2 = f32[256,32]{0,1:T(8,128)S(1)} copy-done((f32[256,32]{0,1:T(8,128)S(1)}, f32[256,32]{0,1:T(8,128)}, u32[]{:S(2)}) %copy-start.2) | copy-done | bytes 32792
  3.3 0.0 copy-start.3
  3.3 0.7 %copy-done.3 = f32[32]{0:T(128)S(1)} copy-done((f32[32]{0:T(128)S(1)}, f32[32]{0:T(128)}, u32[]{:S(2)}) %copy-start.3) | copy-done | bytes 152
  3.9 0.0 copy-start.4
  3.9 0.7 %copy-done.4 = f32[32]{0:T(128)S(1)} copy-done((f32[32]{0:T(128)S(1)}, f32[32]{0:T(128)}, u32[]{:S(2)}) %copy-start.4) | copy-done | bytes 152
  4.6 35.1 %shard_map.55 = bf16[256,4096]{1,0:T(8,128)(2,1)S(1)} custom-call(bf16[256,4352]{1,0:T(8,128)(2,1)S(1)} %copy-done, f32[4,4352]{1,0:T(4,128)S(1)} %copy-done.1, f32[32,256]{1,0:T(8,128)S(1)} %bitcast.2, f32[1,32]{1,0:T(1,128)S(1)} %bitcast.3, f32[32]{0:T(128)S(1)} %copy-done.4), custom_call_target="tpu_custom_call" | custom-call | tf_op jit(solution)/shard_map/pallas_call | solution.py:301
  39.7 1.3 %copy.7 = bf16[256,4096]{1,0:T(8,128)(2,1)} copy(bf16[256,4096]{1,0:T(8,128)(2,1)S(1)} %shard_map.55) | data formatting | bytes 4194304
Async XLA Ops:
  0.0 1.6 %copy-start = (bf16[256,4352]{1,0:T(8,128)(2,1)S(1)}, bf16[256,4352]{1,0:T(8,128)(2,1)}, u32[]{:S(2)}) copy-start(bf16[256,4352]{1,0:T(8,128)(2,1)} %x_ref.1) | copy-start | bytes 6684676
  1.6 0.9 %copy-start.1 = (f32[4,4352]{1,0:T(4,128)S(1)}, f32[4,4352]{1,0:T(4,128)}, u32[]{:S(2)}) copy-start(f32[4,4352]{1,0:T(4,128)} %w_ref.1) | copy-start | bytes 208900
  2.5 0.8 %copy-start.2 = (f32[256,32]{0,1:T(8,128)S(1)}, f32[256,32]{0,1:T(8,128)}, u32[]{:S(2)}) copy-start(f32[256,32]{0,1:T(8,128)} %param.7) | copy-start | bytes 98308
  3.3 0.7 %copy-start.3 = (f32[32]{0:T(128)S(1)}, f32[32]{0:T(128)}, u32[]{:S(2)}) copy-start(f32[32]{0:T(128)} %param.8) | copy-start | bytes 388
  3.9 0.7 %copy-start.4 = (f32[32]{0:T(128)S(1)}, f32[32]{0:T(128)}, u32[]{:S(2)}) copy-start(f32[32]{0:T(128)} %skip_ref.1) | copy-start | bytes 388

commit v2 on v1

--- a/solution.py
+++ b/solution.py
@@ -23,8 +23,9 @@
 
 def kernel(
     n_seq, heads, rows, taps,
-    x_ref, w_ref, sl_ref, dl_ref, skip_ref, out_ref,
-    halo, ext, act, b_t, c_act, scores, tail_tab, cum_tab, rowg, tot,
+    x_hbm, w_hbm, sl_hbm, dl_hbm, skip_hbm, out_ref,
+    x_ref, w_ref, sl_ref, dl_ref, skip_ref, load_sems,
+    gains, halo, ext, act, b_t, c_act, scores, tail_tab, cum_tab, rowg, tot,
     s_send, s_own, s_recv, t_own, t_send, t_recv, p_send, p_recv, e_send, e_recv, ent, local,
     halo_sems, tot_sems, s_sems, t_sems, p_sems, e_sems,
 ):
@@ -48,6 +49,21 @@
     def dev(seq_index):
         return (grp, seq_index)
 
+    loads = [
+        pltpu.make_async_copy(source, target, load_sems.at[k])
+        for k, (source, target) in enumerate(
+            (
+                (sl_hbm, sl_ref),
+                (dl_hbm, dl_ref),
+                (skip_hbm, skip_ref),
+                (w_hbm, w_ref),
+                (x_hbm, x_ref),
+            )
+        )
+    ]
+    for load in loads:
+        load.start()
+
     barrier = pltpu.get_barrier_semaphore()
     for r in (1, 2, 3):
         pl.semaphore_signal(barrier, inc=1, device_id=dev(xor_peer(r)), device_id_type=MESH)
@@ -82,12 +98,14 @@
         )
 
     def halo_copy():
-        return remote(x_ref.at[pl.ds(rows - 16, 16)], halo, halo_sems, 0, me + 1)
+        return remote(x_hbm.at[pl.ds(rows - 8, 8)], halo, halo_sems, 0, me + 1)
 
     @pl.when(me < n_seq - 1)
     def _():
         halo_copy().start()
 
+    for load in loads[:3]:
+        load.wait()
     step = softplus(sl_ref[...])
     eye = lax.broadcasted_iota(jnp.int32, (heads, heads), 0) == lax.broadcasted_iota(
         jnp.int32, (heads, heads), 1
@@ -100,12 +118,11 @@
         step * rate, upto, preferred_element_type=F32, precision=lax.Precision.HIGHEST
     )
     cum_end = cum_t[:, rows - 1 : rows]
-    for h in range(heads):
-        tot[0, h // 2 : h // 2 + 1, pl.ds((h % 2) * HEADDIM, HEADDIM)] = jnp.broadcast_to(
-            cum_end[h : h + 1, :], (1, HEADDIM)
-        )
+    tot[0] = jnp.broadcast_to(cum_end, (heads, HEADDIM))
     for r in (1, 2, 3):
         remote(tot.at[0], tot.at[r], tot_sems, r, xor_peer(r)).start()
+    gain = jnp.sum(jnp.where(eye, skip_ref[...], 0.0), axis=1, keepdims=True)
+    gains[...] = jnp.broadcast_to(gain, (heads, HEADDIM))
     rowg[...] = cum_t - jnp.log(step)
     cum = jnp.transpose(cum_t)
     tail = jnp.transpose(jnp.exp(cum_end - cum_t) * step)
@@ -113,6 +130,9 @@
         tail_tab[h] = jnp.broadcast_to(tail[:, h : h + 1], (rows, HEADDIM))
         cum_tab[h] = jnp.broadcast_to(cum[:, h : h + 1], (rows, HEADDIM))
 
+    for load in loads[3:]:
+        load.wait()
+
     @pl.when(me == 0)
     def _():
         halo[...] = jnp.zeros_like(halo)
@@ -123,7 +143,7 @@
 
     def conv(start, slot):
         cols = pl.ds(start, PAIR)
-        ext[slot, 0:8, :] = halo[:, cols].astype(F32)[8:16]
+        ext[slot, 0:8, :] = halo[:, cols].astype(F32)
         ext[slot, 8 : 8 + rows, :] = x_ref[:, cols].astype(F32)
         total = w_ref[0:1, cols] * ext[slot, pl.ds(9 - taps, rows), :]
         for k in range(1, taps):
@@ -164,7 +184,8 @@
         return remote(e_send.at[j], e_recv.at[j], e_sems, j, xor_peer(1))
 
     def logs(r, j):
-        return tot[r, pl.ds(own_first + j, 1), :]
+        h = 2 * (own_first + j)
+        return jnp.concatenate([tot[r, pl.ds(h, 1), :], tot[r, pl.ds(h + 1, 1), :]], axis=1)
 
     def first_state(j):
         return jnp.where(core == 0, s_own[j], s_recv[j].astype(F32))
@@ -235,7 +256,7 @@
             g = rowg[pl.ds(h, 1), :]
             col = cum_tab[h]
             v = act[i, :, lanes]
-            gain = skip_ref[h]
+            gain = gains[pl.ds(h, 1), :]
             top = scores[0:mid, 0:mid] * jnp.exp(jnp.minimum(col[:mid] - g[:, :mid], 0.0))
             low_a = scores[mid:, 0:mid] * jnp.exp(jnp.minimum(col[mid:] - g[:, :mid], 0.0))
             low_b = scores[mid:, mid:] * jnp.exp(jnp.minimum(col[mid:] - g[:, mid:], 0.0))
@@ -301,10 +322,17 @@
     return pl.pallas_call(
         functools.partial(kernel, n_seq, heads, rows, taps),
         out_shape=jax.ShapeDtypeStruct((rows, heads * HEADDIM), BF16),
-        in_specs=[vmem, vmem, vmem, vmem, pl.BlockSpec(memory_space=pltpu.SMEM)],
+        in_specs=[pl.BlockSpec(memory_space=pltpu.HBM)] * 5,
         out_specs=vmem,
         scratch_shapes=[
-            pltpu.VMEM((16, channels), BF16),
+            pltpu.VMEM((rows, channels), BF16),
+            pltpu.VMEM((taps, channels), F32),
+            pltpu.VMEM((heads, rows), F32),
+            pltpu.VMEM((1, heads), F32),
+            pltpu.VMEM((1, heads), F32),
+            pltpu.SemaphoreType.DMA((5,)),
+            pltpu.VMEM((heads, HEADDIM), F32),
+            pltpu.VMEM((8, channels), BF16),
             pltpu.VMEM((2, rows + 8, PAIR), F32),
             pltpu.VMEM((heads // 2, rows, PAIR), BF16),
             pltpu.VMEM((STATE, rows), BF16),
@@ -313,7 +341,7 @@
             pltpu.VMEM((heads, rows, HEADDIM), F32),
             pltpu.VMEM((heads, rows, HEADDIM), F32),
             pltpu.VMEM((heads, rows), F32),
-            pltpu.VMEM((4, heads // 2, PAIR), F32),
+            pltpu.VMEM((4, heads, HEADDIM), F32),
             pltpu.VMEM(chunk, BF16),
             pltpu.VMEM(chunk, F32),
             pltpu.VMEM(chunk, BF16),
@@ -336,7 +364,18 @@
         compiler_params=pltpu.CompilerParams(
             collective_id=0, has_side_effects=True, vmem_limit_bytes=48 * 1024 * 1024
         ),
-    )(conv_input, conv_weight, step_logit.T, decay_log.reshape(1, heads), skip_gain)
+    )(
+        *(
+            pltpu.with_memory_space_constraint(operand, pltpu.HBM)
+            for operand in (
+                conv_input,
+                conv_weight,
+                step_logit.T,
+                decay_log.reshape(1, heads),
+                skip_gain.reshape(1, heads),
+            )
+        )
+    )
 
 
 def solution(mesh):

time: 41.2 us -> 36 us (0.87)
  local copies, waits for them, and re-layouts: 5.9 us -> 1.32 us
  Pallas kernels: 35.1 us -> 34.5 us
    unnamed x11 -> x1, local copies, waits for them, and re-layouts: 5.9 us -> 1.32 us
    pallas_call x1, Pallas kernels: 35.1 us -> 34.5 us  [on_device(): pl.pallas_call(functools.partial(kernel, n_seq, heads, rows, taps), out_s...]
where the time goes in v2:
time: 36 us; the launch traced here: 35.8 us
  Pallas kernels  34.5 us (96%)
  local copies, waits for them, and re-layouts  1.32 us (4%)
    pallas_call x1, Pallas kernels, on_device(): pl.pallas_call(functools.partial(kernel, n_seq, heads, rows, taps), out_s...  34.5 us
    unnamed x1, local copies, waits for them, and re-layouts  1.32 us

profile of v2, /device:TPU:25, one launch (start us, length us, event | category | flops | bytes accessed | tf_op | source)
XLA Modules:
  0.0 35.8 jit_solution(7121406175214676109)
XLA Ops:
  0.0 34.5 %shard_map.55 = bf16[256,4096]{1,0:T(8,128)(2,1)S(1)} custom-call(bf16[256,4352]{1,0:T(8,128)(2,1)} %x_hbm.1, f32[4,4352]{1,0:T(4,128)} %w_hbm.1, f32[32,256]{1,0:T(8,128)} %bitcast.3, f32[1,32]{1,0:T(1,128)} %bitcast.4, f32[1,32]{1,0:T(1,128)} %bitcast.5), custom_call_target="tpu_custom_call" | custom-call | tf_op jit(solution)/shard_map/pallas_call | solution.py:322
  34.5 1.3 %copy.7 = bf16[256,4096]{1,0:T(8,128)(2,1)} copy(bf16[256,4096]{1,0:T(8,128)(2,1)S(1)} %shard_map.55) | data formatting | bytes 4194304

commit v3 on v2

--- a/solution.py
+++ b/solution.py
@@ -25,9 +25,9 @@
     n_seq, heads, rows, taps,
     x_hbm, w_hbm, sl_hbm, dl_hbm, skip_hbm, out_ref,
     x_ref, w_ref, sl_ref, dl_ref, skip_ref, load_sems,
-    gains, halo, ext, act, b_t, c_act, scores, tail_tab, cum_tab, rowg, tot,
-    s_send, s_own, s_recv, t_own, t_send, t_recv, p_send, p_recv, e_send, e_recv, ent, local,
-    halo_sems, tot_sems, s_sems, t_sems, p_sems, e_sems,
+    gains, halo, ext, act, b_t, c_act, scores, tail_tab, cum_tab, rowg, tot, cum_cols, plane,
+    s_send, s_own, s_recv, t_own, t_send, t_recv, p_send, p_recv, g_send, g_recv, e_send, e_recv, ent, local,
+    halo_sems, tot_sems, s_sems, t_sems, p_sems, g_sems, e_sems,
 ):
     me = lax.axis_index("seq")
     grp = lax.axis_index("grp")
@@ -84,13 +84,6 @@
         def _():
             pl.semaphore_signal(barrier, inc=1, device_id=dev(me - 1), device_id_type=MESH)
 
-    next_count = 1 - (quad + 1) // quads
-    prev_count = (quad + quads - 1) // quads
-    pl.semaphore_wait(
-        barrier,
-        3 + next_count * (1 + place // 3) + prev_count * (2 - (place + 3) // 4),
-    )
-
     def remote(src, dst, sems, j, target):
         return pltpu.make_async_remote_copy(
             src_ref=src, dst_ref=dst, send_sem=sems.at[0, j], recv_sem=sems.at[1, j],
@@ -99,10 +92,6 @@
 
     def halo_copy():
         return remote(x_hbm.at[pl.ds(rows - 8, 8)], halo, halo_sems, 0, me + 1)
-
-    @pl.when(me < n_seq - 1)
-    def _():
-        halo_copy().start()
 
     for load in loads[:3]:
         load.wait()
@@ -119,16 +108,27 @@
     )
     cum_end = cum_t[:, rows - 1 : rows]
     tot[0] = jnp.broadcast_to(cum_end, (heads, HEADDIM))
+
+    next_count = 1 - (quad + 1) // quads
+    prev_count = (quad + quads - 1) // quads
+    pl.semaphore_wait(
+        barrier,
+        3 + next_count * (1 + place // 3) + prev_count * (2 - (place + 3) // 4),
+    )
+
+    @pl.when(me < n_seq - 1)
+    def _():
+        halo_copy().start()
+
     for r in (1, 2, 3):
         remote(tot.at[0], tot.at[r], tot_sems, r, xor_peer(r)).start()
     gain = jnp.sum(jnp.where(eye, skip_ref[...], 0.0), axis=1, keepdims=True)
     gains[...] = jnp.broadcast_to(gain, (heads, HEADDIM))
     rowg[...] = cum_t - jnp.log(step)
-    cum = jnp.transpose(cum_t)
+    cum_cols[...] = jnp.transpose(cum_t)
     tail = jnp.transpose(jnp.exp(cum_end - cum_t) * step)
     for h in range(heads):
         tail_tab[h] = jnp.broadcast_to(tail[:, h : h + 1], (rows, HEADDIM))
-        cum_tab[h] = jnp.broadcast_to(cum[:, h : h + 1], (rows, HEADDIM))
 
     for load in loads[3:]:
         load.wait()
@@ -157,11 +157,14 @@
     b_trans = jnp.transpose(b_rows.astype(F32)).astype(BF16)
     b_t[...] = b_trans
     c_act[...] = c_rows
-    raw = jnp.dot(c_rows, b_trans, preferred_element_type=F32)
-    scores[...] = jnp.where(row_id >= col_id, raw, 0.0)
 
     own_first = half * core
     other_first = half * (1 - core)
+    steps = half // 2
+
+    def pair_of(first, j):
+        flip = 1 - j % 2
+        return first + steps * (side + flip * (1 - 2 * side)) + j // 2
 
     def pair_state(i, slot):
         a = conv(pl.multiple_of(i * PAIR, PAIR), slot)
@@ -174,78 +177,76 @@
     def s_copy(j):
         return remote(s_send.at[j], s_recv.at[j], s_sems, j, xor_peer(1))
 
-    def t_copy(j):
-        return remote(t_send.at[j], t_recv.at[j], t_sems, j, xor_peer(2))
-
-    def p_copy(j):
-        return remote(p_send.at[j], p_recv.at[j], p_sems, j, me + 4)
+    def t_copy(m):
+        return remote(t_send.at[m], t_recv.at[m], t_sems, m, xor_peer(2))
+
+    def p_copy(m):
+        return remote(p_send.at[m], p_recv.at[m], p_sems, m, me + 4)
+
+    def g_copy(m):
+        return remote(g_send.at[m], g_recv.at[m], g_sems, m, xor_peer(2))
 
     def e_copy(j):
         return remote(e_send.at[j], e_recv.at[j], e_sems, j, xor_peer(1))
 
     def logs(r, j):
-        h = 2 * (own_first + j)
+        h = 2 * pair_of(own_first, j)
         return jnp.concatenate([tot[r, pl.ds(h, 1), :], tot[r, pl.ds(h + 1, 1), :]], axis=1)
 
-    def first_state(j):
-        return jnp.where(core == 0, s_own[j], s_recv[j].astype(F32))
-
-    def chip_step(j):
+    def local_states(j):
+        s_send[j] = pair_state(pair_of(other_first, j), 0).astype(BF16)
+        s_copy(j).start()
+        s_own[j] = pair_state(pair_of(own_first, j), 1)
+
+    def chip_total(j):
         s_copy(j).wait_recv()
         mine, got = s_own[j], s_recv[j].astype(F32)
         decay_last = jnp.exp(jnp.where(core == 0, logs(1, j), logs(0, j)))
-        total = decay_last * jnp.where(core == 0, mine, got) + jnp.where(core == 0, got, mine)
-        t_own[j] = total
-        t_send[j] = total.astype(BF16)
-        t_copy(j).start()
+        return decay_last * jnp.where(core == 0, mine, got) + jnp.where(core == 0, got, mine)
+
+    def core_step(j, e_chip):
+        decay_first = jnp.exp(jnp.where(core == 0, logs(0, j), logs(1, j)))
+        first = jnp.where(core == 0, s_own[j], s_recv[j].astype(F32))
+        e_second = decay_first * e_chip + first
+        e_send[j] = jnp.where(core == 0, e_second, e_chip).astype(BF16)
+        e_copy(j).start()
+        ent[j] = jnp.where(core == 0, e_chip, e_second).astype(BF16)
 
     for r in (1, 2, 3):
         remote(tot.at[0], tot.at[r], tot_sems, r, xor_peer(r)).wait_recv()
 
-    @pl.loop(0, half)
-    def _(j):
-        s_send[j] = pair_state(other_first + j, 0).astype(BF16)
-        s_copy(j).start()
-        s_own[j] = pair_state(own_first + j, 1)
-
-        @pl.when(j >= 1)
-        def _():
-            chip_step(j - 1)
-
-    chip_step(half - 1)
-
-    def quad_step(j):
-        t_copy(j).wait_recv()
-        mine, got = t_own[j], t_recv[j].astype(F32)
+    def quad_step(m):
+        j = 2 * m + 1
+        t_copy(m).wait_recv()
+        mine, got = t_own[m], t_recv[m].astype(F32)
         log_mine = logs(0, j) + logs(1, j)
         log_got = logs(2, j) + logs(3, j)
         log_0 = jnp.where(side == 0, log_mine, log_got)
         log_1 = jnp.where(side == 0, log_got, log_mine)
         t_0 = jnp.where(side == 0, mine, got)
         t_1 = jnp.where(side == 0, got, mine)
-        plane = jnp.exp(log_1) * t_0 + t_1
+        t_own[m] = t_0
+        plane[...] = jnp.exp(log_1) * t_0 + t_1
 
         @pl.when(has_prev)
         def _():
-            p_copy(j).wait_recv()
+            p_copy(m).wait_recv()
 
         @pl.when(quad == 0)
         def _():
-            p_recv[j] = jnp.zeros((STATE, PAIR), BF16)
-
-        before = p_recv[j].astype(F32)
+            p_recv[m] = jnp.zeros((STATE, PAIR), BF16)
+
+        before = p_recv[m].astype(F32)
 
         @pl.when(has_next)
         def _():
-            p_send[j] = (jnp.exp(log_0 + log_1) * before + plane).astype(BF16)
-            p_copy(j).start()
-
-        e_chip = jnp.where(side == 0, before, jnp.exp(log_0) * before + t_0)
-        decay_first = jnp.exp(jnp.where(core == 0, logs(0, j), logs(1, j)))
-        e_second = decay_first * e_chip + first_state(j)
-        e_send[j] = jnp.where(core == 0, e_second, e_chip).astype(BF16)
-        e_copy(j).start()
-        ent[j] = jnp.where(core == 0, e_chip, e_second).astype(BF16)
+            p_send[m] = (jnp.exp(log_0 + log_1) * before + plane[...]).astype(BF16)
+            p_copy(m).start()
+
+        e_second = jnp.exp(log_0) * before + t_own[m]
+        g_send[m] = jnp.where(side == 0, e_second, before).astype(BF16)
+        g_copy(m).start()
+        core_step(j, jnp.where(side == 0, before, e_second))
 
     mid = rows // 2
 
@@ -274,21 +275,63 @@
         ).astype(out_ref.dtype)
 
     def finish_step(j):
-        finish(own_first + j, ent[j])
+        finish(pair_of(own_first, j), ent[j])
         e_copy(j).wait_recv()
-        finish(other_first + j, e_recv[j])
-
-    @pl.loop(0, half)
-    def _(j):
-        quad_step(j)
-        intra(own_first + j)
-        intra(other_first + j)
-
-        @pl.when(j >= 1)
-        def _():
-            finish_step(j - 1)
-
-    finish_step(half - 1)
+        finish(pair_of(other_first, j), e_recv[j])
+
+    most = 2 * steps
+    lag = jnp.minimum(steps - 2 + 2 * quad, most)
+
+    @pl.loop(0, most + steps + 2)
+    def _(t):
+        @pl.when((t >= 1) & (t < steps + 1))
+        def _():
+            t_send[t - 1] = chip_total(2 * t - 2).astype(BF16)
+            t_copy(t - 1).start()
+
+        @pl.when(t < steps)
+        def _():
+            local_states(2 * t)
+
+        @pl.when((t >= 1) & (t < steps + 1))
+        def _():
+            t_own[t - 1] = chip_total(2 * t - 1)
+
+        @pl.when((t >= lag) & (t < lag + steps))
+        def _():
+            quad_step(t - lag)
+
+        @pl.when((t >= lag + 1) & (t < lag + 1 + steps))
+        def _():
+            m = t - lag - 1
+            g_copy(m).wait_recv()
+            core_step(2 * m, g_recv[m].astype(F32))
+
+        @pl.when(t < steps)
+        def _():
+            local_states(2 * t + 1)
+
+        @pl.when(t == steps)
+        def _():
+            raw = jnp.dot(c_act[...], b_t[...], preferred_element_type=F32)
+            scores[...] = jnp.where(row_id >= col_id, raw, 0.0)
+            cum = cum_cols[...]
+            for h in range(heads):
+                cum_tab[h] = jnp.broadcast_to(cum[:, h : h + 1], (rows, HEADDIM))
+
+        @pl.when((t >= steps) & (t < 2 * steps))
+        def _():
+            @pl.loop(0, 2)
+            def _(u):
+                j = 2 * (t - steps) + u
+                intra(pair_of(own_first, j))
+                intra(pair_of(other_first, j))
+
+        @pl.when((t >= lag + 2) & (t < lag + 2 + steps))
+        def _():
+            m = t - lag - 2
+            finish_step(2 * m + 1)
+            finish_step(2 * m)
 
     @pl.when(me < n_seq - 1)
     def _():
@@ -300,12 +343,16 @@
     @pl.loop(0, half)
     def _(j):
         s_copy(j).wait_send()
-        t_copy(j).wait_send()
         e_copy(j).wait_send()
 
+    @pl.loop(0, steps)
+    def _(m):
+        t_copy(m).wait_send()
+        g_copy(m).wait_send()
+
         @pl.when(has_next)
         def _():
-            p_copy(j).wait_send()
+            p_copy(m).wait_send()
 
 
 def on_device(n_seq, conv_input, conv_weight, step_logit, decay_log, skip_gain):
@@ -315,6 +362,7 @@
     half = heads // 4
     vmem = pl.BlockSpec(memory_space=pltpu.VMEM)
     chunk = (half, STATE, PAIR)
+    part = (half // 2, STATE, PAIR)
 
     def pair_sems(count):
         return pltpu.SemaphoreType.DMA((2, count))
@@ -342,14 +390,18 @@
             pltpu.VMEM((heads, rows, HEADDIM), F32),
             pltpu.VMEM((heads, rows), F32),
             pltpu.VMEM((4, heads, HEADDIM), F32),
+            pltpu.VMEM((rows, heads), F32),
+            pltpu.VMEM((STATE, PAIR), F32),
             pltpu.VMEM(chunk, BF16),
             pltpu.VMEM(chunk, F32),
             pltpu.VMEM(chunk, BF16),
-            pltpu.VMEM(chunk, F32),
-            pltpu.VMEM(chunk, BF16),
-            pltpu.VMEM(chunk, BF16),
-            pltpu.VMEM(chunk, BF16),
-            pltpu.VMEM(chunk, BF16),
+            pltpu.VMEM(part, F32),
+            pltpu.VMEM(part, BF16),
+            pltpu.VMEM(part, BF16),
+            pltpu.VMEM(part, BF16),
+            pltpu.VMEM(part, BF16),
+            pltpu.VMEM(part, BF16),
+            pltpu.VMEM(part, BF16),
             pltpu.VMEM(chunk, BF16),
             pltpu.VMEM(chunk, BF16),
             pltpu.VMEM(chunk, BF16),
@@ -357,8 +409,9 @@
             pair_sems(1),
             pair_sems(4),
             pair_sems(half),
-            pair_sems(half),
-            pair_sems(half),
+            pair_sems(half // 2),
+            pair_sems(half // 2),
+            pair_sems(half // 2),
             pair_sems(half),
         ],
         compiler_params=pltpu.CompilerParams(

time: 36 us -> 34.2 us (0.950)
  Pallas kernels: 34.5 us -> 32.6 us
    pallas_call x1, Pallas kernels: 34.5 us -> 32.6 us  [on_device(): pl.pallas_call(functools.partial(kernel, n_seq, heads, rows, taps), out_s...]
where the time goes in v3:
time: 34.2 us; the launch traced here: 33.9 us
  Pallas kernels  32.6 us (95%)
  local copies, waits for them, and re-layouts  1.32 us (4%)
    pallas_call x1, Pallas kernels, on_device(): pl.pallas_call(functools.partial(kernel, n_seq, heads, rows, taps), out_s...  32.6 us
    unnamed x1, local copies, waits for them, and re-layouts  1.32 us

profile of v3, /device:TPU:25, one launch (start us, length us, event | category | flops | bytes accessed | tf_op | source)
XLA Modules:
  0.0 33.9 jit_solution(2095876659542410231)
XLA Ops:
  0.0 32.6 %shard_map.55 = bf16[256,4096]{1,0:T(8,128)(2,1)S(1)} custom-call(bf16[256,4352]{1,0:T(8,128)(2,1)} %x_hbm.1, f32[4,4352]{1,0:T(4,128)} %w_hbm.1, f32[32,256]{1,0:T(8,128)} %bitcast.3, f32[1,32]{1,0:T(1,128)} %bitcast.4, f32[1,32]{1,0:T(1,128)} %bitcast.5), custom_call_target="tpu_custom_call" | custom-call | tf_op jit(solution)/shard_map/pallas_call | solution.py:370
  32.6 1.3 %copy.7 = bf16[256,4096]{1,0:T(8,128)(2,1)} copy(bf16[256,4096]{1,0:T(8,128)(2,1)S(1)} %shard_map.55) | data formatting | bytes 4194304

commit v4 on v3

--- a/solution.py
+++ b/solution.py
@@ -95,6 +95,17 @@
 
     for load in loads[:3]:
         load.wait()
+    next_count = 1 - (quad + 1) // quads
+    prev_count = (quad + quads - 1) // quads
+    pl.semaphore_wait(
+        barrier,
+        3 + next_count * (1 + place // 3) + prev_count * (2 - (place + 3) // 4),
+    )
+
+    @pl.when(me < n_seq - 1)
+    def _():
+        halo_copy().start()
+
     step = softplus(sl_ref[...])
     eye = lax.broadcasted_iota(jnp.int32, (heads, heads), 0) == lax.broadcasted_iota(
         jnp.int32, (heads, heads), 1
@@ -108,17 +119,6 @@
     )
     cum_end = cum_t[:, rows - 1 : rows]
     tot[0] = jnp.broadcast_to(cum_end, (heads, HEADDIM))
-
-    next_count = 1 - (quad + 1) // quads
-    prev_count = (quad + quads - 1) // quads
-    pl.semaphore_wait(
-        barrier,
-        3 + next_count * (1 + place // 3) + prev_count * (2 - (place + 3) // 4),
-    )
-
-    @pl.when(me < n_seq - 1)
-    def _():
-        halo_copy().start()
 
     for r in (1, 2, 3):
         remote(tot.at[0], tot.at[r], tot_sems, r, xor_peer(r)).start()
@@ -280,7 +280,9 @@
         finish(pair_of(other_first, j), e_recv[j])
 
     most = 2 * steps
-    lag = jnp.minimum(steps - 2 + 2 * quad, most)
+    lag = jnp.minimum(steps - 2 + (3 * quad + 1) // 2, most)
+    begin = steps + 2 * (1 - prev_count)
+    end_lag = jnp.maximum(lag + 2, begin)
 
     @pl.loop(0, most + steps + 2)
     def _(t):
@@ -311,7 +313,7 @@
         def _():
             local_states(2 * t + 1)
 
-        @pl.when(t == steps)
+        @pl.when(t == begin)
         def _():
             raw = jnp.dot(c_act[...], b_t[...], preferred_element_type=F32)
             scores[...] = jnp.where(row_id >= col_id, raw, 0.0)
@@ -319,17 +321,17 @@
             for h in range(heads):
                 cum_tab[h] = jnp.broadcast_to(cum[:, h : h + 1], (rows, HEADDIM))
 
-        @pl.when((t >= steps) & (t < 2 * steps))
+        @pl.when((t >= begin) & (t < begin + steps))
         def _():
             @pl.loop(0, 2)
             def _(u):
-                j = 2 * (t - steps) + u
+                j = 2 * (t - begin) + u
                 intra(pair_of(own_first, j))
                 intra(pair_of(other_first, j))
 
-        @pl.when((t >= lag + 2) & (t < lag + 2 + steps))
-        def _():
-            m = t - lag - 2
+        @pl.when((t >= end_lag) & (t < end_lag + steps))
+        def _():
+            m = t - end_lag
             finish_step(2 * m + 1)
             finish_step(2 * m)
 

time: 34.2 us -> 34.5 us (level)
  Pallas kernels: 32.6 us -> 33.1 us
    pallas_call x1, Pallas kernels: 32.6 us -> 33.1 us  [on_device(): pl.pallas_call(functools.partial(kernel, n_seq, heads, rows, taps), out_s...]
where the time goes in v4:
time: 34.5 us; the launch traced here: 34.4 us
  Pallas kernels  33.1 us (96%)
  local copies, waits for them, and re-layouts  1.32 us (4%)
    pallas_call x1, Pallas kernels, on_device(): pl.pallas_call(functools.partial(kernel, n_seq, heads, rows, taps), out_s...  33.1 us
    unnamed x1, local copies, waits for them, and re-layouts  1.32 us

profile of v4, /device:TPU:25, one launch (start us, length us, event | category | flops | bytes accessed | tf_op | source)
XLA Modules:
  0.0 34.4 jit_solution(5986533011992507266)
XLA Ops:
  0.0 33.1 %shard_map.55 = bf16[256,4096]{1,0:T(8,128)(2,1)S(1)} custom-call(bf16[256,4352]{1,0:T(8,128)(2,1)} %x_hbm.1, f32[4,4352]{1,0:T(4,128)} %w_hbm.1, f32[32,256]{1,0:T(8,128)} %bitcast.3, f32[1,32]{1,0:T(1,128)} %bitcast.4, f32[1,32]{1,0:T(1,128)} %bitcast.5), custom_call_target="tpu_custom_call" | custom-call | tf_op jit(solution)/shard_map/pallas_call | solution.py:372
  33.1 1.3 %copy.7 = bf16[256,4096]{1,0:T(8,128)(2,1)} copy(bf16[256,4096]{1,0:T(8,128)(2,1)S(1)} %shard_map.55) | data formatting | bytes 4194304

commit v5 on v3

--- a/solution.py
+++ b/solution.py
@@ -57,7 +57,8 @@
                 (dl_hbm, dl_ref),
                 (skip_hbm, skip_ref),
                 (w_hbm, w_ref),
-                (x_hbm, x_ref),
+                (x_hbm.at[:, inner:], x_ref.at[:, inner:]),
+                (x_hbm.at[:, :inner], x_ref.at[:, :inner]),
             )
         )
     ]
@@ -130,7 +131,7 @@
     for h in range(heads):
         tail_tab[h] = jnp.broadcast_to(tail[:, h : h + 1], (rows, HEADDIM))
 
-    for load in loads[3:]:
+    for load in loads[3:5]:
         load.wait()
 
     @pl.when(me == 0)
@@ -145,13 +146,14 @@
         cols = pl.ds(start, PAIR)
         ext[slot, 0:8, :] = halo[:, cols].astype(F32)
         ext[slot, 8 : 8 + rows, :] = x_ref[:, cols].astype(F32)
-        total = w_ref[0:1, cols] * ext[slot, pl.ds(9 - taps, rows), :]
+        total = (0.5 * w_ref[0:1, cols]) * ext[slot, pl.ds(9 - taps, rows), :]
         for k in range(1, taps):
-            total = total + w_ref[k : k + 1, cols] * ext[slot, pl.ds(9 - taps + k, rows), :]
-        half_v = 0.5 * total
+            total = total + (0.5 * w_ref[k : k + 1, cols]) * ext[slot, pl.ds(9 - taps + k, rows), :]
+        half_v = total
         return (half_v + half_v * jnp.tanh(half_v)).astype(BF16)
 
     maps = conv(inner, 0)
+    loads[5].wait()
     b_rows = maps[:, :STATE]
     c_rows = maps[:, STATE:]
     b_trans = jnp.transpose(b_rows.astype(F32)).astype(BF16)
@@ -211,9 +213,6 @@
         e_send[j] = jnp.where(core == 0, e_second, e_chip).astype(BF16)
         e_copy(j).start()
         ent[j] = jnp.where(core == 0, e_chip, e_second).astype(BF16)
-
-    for r in (1, 2, 3):
-        remote(tot.at[0], tot.at[r], tot_sems, r, xor_peer(r)).wait_recv()
 
     def quad_step(m):
         j = 2 * m + 1
@@ -284,6 +283,11 @@
 
     @pl.loop(0, most + steps + 2)
     def _(t):
+        @pl.when(t == 1)
+        def _():
+            for r in (1, 2, 3):
+                remote(tot.at[0], tot.at[r], tot_sems, r, xor_peer(r)).wait_recv()
+
         @pl.when((t >= 1) & (t < steps + 1))
         def _():
             t_send[t - 1] = chip_total(2 * t - 2).astype(BF16)
@@ -378,7 +382,7 @@
             pltpu.VMEM((heads, rows), F32),
             pltpu.VMEM((1, heads), F32),
             pltpu.VMEM((1, heads), F32),
-            pltpu.SemaphoreType.DMA((5,)),
+            pltpu.SemaphoreType.DMA((6,)),
             pltpu.VMEM((heads, HEADDIM), F32),
             pltpu.VMEM((8, channels), BF16),
             pltpu.VMEM((2, rows + 8, PAIR), F32),

time: 34.2 us -> 34 us (level)
  no operation moved by 1% of the time
where the time goes in v5:
time: 34 us; the launch traced here: 33.7 us
  Pallas kernels  32.4 us (95%)
  local copies, waits for them, and re-layouts  1.32 us (4%)
    pallas_call x1, Pallas kernels, on_device(): pl.pallas_call(functools.partial(kernel, n_seq, heads, rows, taps), out_s...  32.4 us
    unnamed x1, local copies, waits for them, and re-layouts  1.32 us

profile of v5, /device:TPU:25, one launch (start us, length us, event | category | flops | bytes accessed | tf_op | source)
XLA Modules:
  0.0 33.7 jit_solution(16843937680744059861)
XLA Ops:
  0.0 32.4 %shard_map.55 = bf16[256,4096]{1,0:T(8,128)(2,1)S(1)} custom-call(bf16[256,4352]{1,0:T(8,128)(2,1)} %x_hbm.1, f32[4,4352]{1,0:T(4,128)} %w_hbm.1, f32[32,256]{1,0:T(8,128)} %bitcast.3, f32[1,32]{1,0:T(1,128)} %bitcast.4, f32[1,32]{1,0:T(1,128)} %bitcast.5), custom_call_target="tpu_custom_call" | custom-call | tf_op jit(solution)/shard_map/pallas_call | solution.py:374
  32.4 1.3 %copy.7 = bf16[256,4096]{1,0:T(8,128)(2,1)} copy(bf16[256,4096]{1,0:T(8,128)(2,1)S(1)} %shard_map.55) | data formatting | bytes 4194304
